TPU v7x, 128 devices: a whole 4x4x4 slice. The times are simulated.
128 devices in a mesh: patch: 16 (over y, x), col: 8 (over z, core).
Axes of the slice: x: 4, y: 4, z: 4, core: 2. Of those that a mesh axis runs over, the one named last changes fastest.
Arguments:
- potential0: float32 [512, 16, 128], P(('patch', 'col')), may hold values from -3 to 3
- source_term: float32 [512, 16, 128], P(('patch', 'col')), may hold values from -9 to 9
- self_coef: float32 [512, 128], P(('patch', 'col')), may hold values from 1 to 4
- nearfield: float32 [512, 24, 128, 128], P(('patch', 'col')), may hold values from -0.109375 to 0.109375
- precond: float32 [512, 128, 128], P(('patch', 'col')), may hold values from -1 to 2
- exch_current: float32 [512, 128], P(('patch', 'col')), may hold values from 0.05 to 0.5
- conductance: float32 [512, 128], P(('patch', 'col')), may hold values from 0.1 to 1
- member: int32 [512, 128], P(('patch', 'col')), may hold values from 0 to 63
- anode_drive: float32 [64], replicated, may hold values from -1 to 1
- pair_source: int32 [512, 24], P(('patch', 'col')), may hold values from 0 to 39
- pair_count: int32 [512], P(('patch', 'col')), may hold values from 1 to 24, as said below
Outputs:
- potential: float32 [512, 16, 128], P(('patch', 'col'))
- residual: float32 [512, 16, 128], P(('patch', 'col'))
Inputs may be any that keep to these rules, and one draw needn't show every extreme that they name: Slots k < pair_count[b] of block b are live; some block has all 24 slots live, and the blocks of some devices hold far more live pairs than those of others.
All inputs are finite; a program needn't handle non-finite values.
Results may differ from a plain program's by a relative error of at most 0.0003.
Values sent between devices are 32-bit elements; how exact they have to be, the bound alone decides.
A program may use at most 64 MiB of HBM per device.

v0:
```python
import jax
import jax.numpy as jnp
from jax import lax
from jax.sharding import PartitionSpec as P

NEWTON = 2
GMRES = 2
ALPHA = 0.6
BETA = 0.4
EPS = 1e-06


def from_behind(array, axis, by):
    size = lax.axis_size(axis)
    return lax.ppermute(array, axis, [(i, (i + by) % size) for i in range(size)])


def column_sum(left, right):
    return jnp.sum(left * right, axis=(0, 2))


def least_squares(columns, beta):
    depth = len(columns)
    hessen = jnp.zeros((beta.shape[0], depth + 1, depth), jnp.float32)
    for place in range(depth):
        hessen = hessen.at[:, : place + 2, place].set(columns[place].T)
    gram = jnp.einsum("cij,cik->cjk", hessen, hessen, precision=lax.Precision.HIGHEST)
    right = beta[:, None] * hessen[:, 0, :]
    lower = jnp.linalg.cholesky(gram)
    middle = jax.scipy.linalg.solve_triangular(lower, right[:, :, None], lower=True)
    return jax.scipy.linalg.solve_triangular(lower, middle, lower=True, trans=1)[:, :, 0]


def body(
    potential0,
    source_term,
    self_coef,
    nearfield,
    precond,
    exch_current,
    conductance,
    member,
    anode_drive,
    pair_source,
    pair_count,
):
    pair_slots = pair_source.shape[1]
    live_mask = (jnp.arange(pair_slots, dtype=jnp.int32)[None, :] < pair_count[:, None]).astype(
        jnp.float32
    )
    members = anode_drive.shape[0]
    onehot = (jnp.arange(members, dtype=jnp.int32)[:, None, None] == member[None]).astype(
        jnp.float32
    )
    member_drive = jnp.sum(onehot * anode_drive[:, None, None], axis=0)
    diagonal = self_coef[:, None, :]
    current = exch_current[:, None, :]
    conduct = conductance[:, None, :]

    def near_field(field):
        own_patch = lax.all_gather(field, "col", axis=0, tiled=True)
        before = from_behind(field, "patch", 1)
        following = from_behind(field, "patch", -1)
        stacked = jnp.concatenate([own_patch, before, following], axis=0)
        sources = stacked[pair_source]
        return jnp.einsum(
            "bkij,bkcj->bci",
            nearfield,
            sources * live_mask[:, :, None, None],
            precision=lax.Precision.HIGHEST,
        )

    def mismatch(field, near_value):
        grow = jnp.exp(ALPHA * field)
        shrink = jnp.exp(-BETA * field)
        value = (
            diagonal * field
            + near_value
            + current * (grow - shrink)
            + conduct * (field - member_drive[:, None, :])
            - source_term
        )
        slope = current * (ALPHA * grow + BETA * shrink) + conduct
        return (value, slope)

    field = potential0
    near_now = near_field(field)
    for newton in range(NEWTON):
        value, slope = mismatch(field, near_now)
        start = -value
        beta = jnp.sqrt(lax.psum(column_sum(start, start), ("patch", "col")) + EPS)
        basis = [start / beta[None, :, None]]
        directions = []
        near_images = []
        columns = []
        for step in range(GMRES):
            direction = jnp.einsum(
                "bij,bcj->bci", precond, basis[step], precision=lax.Precision.HIGHEST
            )
            directions.append(direction)
            near_image = near_field(direction)
            near_images.append(near_image)
            image = diagonal * direction + near_image + slope * direction
            coeffs = []
            for place in range(step + 1):
                coeff = lax.psum(column_sum(basis[place], image), ("patch", "col"))
                image = image - coeff[None, :, None] * basis[place]
                coeffs.append(coeff)
            norm = jnp.sqrt(lax.psum(column_sum(image, image), ("patch", "col")) + EPS)
            basis.append(image / norm[None, :, None])
            columns.append(jnp.stack(coeffs + [norm]))
        weights = least_squares(columns, beta)
        update = jnp.zeros_like(field)
        for step in range(GMRES):
            update = update + weights[:, step][None, :, None] * directions[step]
        field = field + update
        near_now = near_field(field)
    final_value, final_slope = mismatch(field, near_now)
    return (field, final_value)


def solution(mesh):
    return jax.shard_map(
        body,
        mesh=mesh,
        in_specs=(
            P(("patch", "col"), None, None),
            P(("patch", "col"), None, None),
            P(("patch", "col"), None),
            P(("patch", "col"), None, None, None),
            P(("patch", "col"), None, None),
            P(("patch", "col"), None),
            P(("patch", "col"), None),
            P(("patch", "col"), None),
            P(),
            P(("patch", "col"), None),
            P(("patch", "col")),
        ),
        out_specs=(P(("patch", "col"), None, None), P(("patch", "col"), None, None)),
        check_vma=False,
    )
```

profile of v0, /device:TPU:1, one launch (start us, length us, event | category | flops | bytes accessed | tf_op | source)
XLA Modules:
  0.0 974.0 jit_solution(4111155873102971596)
XLA Ops:
  0.7 2.1 collective-permute-start
  2.8 3.8 collective-permute-start.1
  6.6 15.1 %all_gather.21 = f32[32,16,128]{2,1,0:T(8,128)S(1)} all-gather(f32[4,16,128]{2,1,0:T(8,128)} %param.24), channel_id=1, replica_groups=mesh['patch'=16,'col'=8] {'col'}, dimensions={0}, use_global_device_ids=true | all-gather | bytes 294912 | tf_op jit(solution)/shard_map/all_gather | solution.py:61
  22.5 0.7 fusion.40
  23.2 0.8 select_reduce_fusion
  24.0 0.7 gather_fusion
  24.7 7.6 multiply_reduce_fusion.11
  32.3 64.2 %psum.84 = f32[16]{0:T(128)S(1)} all-reduce(f32[16]{0:T(128)S(1)} %get-tuple-element.61), channel_id=1, replica_groups=mesh['patch'=16,'col'=8] {'patch','col'}, use_global_device_ids=true, to_apply=%region_2.0 | all-reduce | flops 16 | bytes 128 | tf_op jit(solution)/shard_map/psum | solution.py:91
  97.3 4.6 collective-permute-start.3
  101.9 13.9 %all_gather.22 = f32[32,16,128]{2,1,0:T(8,128)S(1)} all-gather(f32[4,16,128]{2,1,0:T(8,128)S(1)} %fusion.43), channel_id=1, replica_groups=mesh['patch'=16,'col'=8] {'col'}, dimensions={0}, use_global_device_ids=true | all-gather | bytes 294912 | tf_op jit(solution)/shard_map/all_gather | solution.py:61
  115.8 0.7 gather_fusion.1
  116.5 7.5 multiply_reduce_fusion.10
  124.0 63.4 %psum.85 = f32[16]{0:T(128)S(1)} all-reduce(f32[16]{0:T(128)S(1)} %get-tuple-element.63), channel_id=1, replica_groups=mesh['patch'=16,'col'=8] {'patch','col'}, use_global_device_ids=true, to_apply=%region_4.0 | all-reduce | flops 16 | bytes 128 | tf_op jit(solution)/shard_map/psum | solution.py:106
  187.6 63.0 %psum.86 = f32[16]{0:T(128)S(1)} all-reduce(f32[16]{0:T(128)S(1)} %multiply_reduce_fusion.9), channel_id=1, replica_groups=mesh['patch'=16,'col'=8] {'patch','col'}, use_global_device_ids=true, to_apply=%region_6.0 | all-reduce | flops 16 | bytes 128 | tf_op jit(solution)/shard_map/psum | solution.py:109
  251.2 0.8 collective-permute-start.4
  252.1 4.0 collective-permute-start.5
  256.0 13.8 %all_gather.23 = f32[32,16,128]{2,1,0:T(8,128)S(1)} all-gather(f32[4,16,128]{2,1,0:T(8,128)S(1)} %fusion.44), channel_id=1, replica_groups=mesh['patch'=16,'col'=8] {'col'}, dimensions={0}, use_global_device_ids=true | all-gather | bytes 294912 | tf_op jit(solution)/shard_map/all_gather | solution.py:61
  269.8 0.7 gather_fusion.2
  270.5 7.5 multiply_reduce_fusion.8
  278.0 64.4 %psum.87 = f32[16]{0:T(128)S(1)} all-reduce(f32[16]{0:T(128)S(1)} %get-tuple-element.65), channel_id=1, replica_groups=mesh['patch'=16,'col'=8] {'patch','col'}, use_global_device_ids=true, to_apply=%region_8.0 | all-reduce | flops 16 | bytes 128 | tf_op jit(solution)/shard_map/psum | solution.py:106
  342.6 62.5 %psum.88 = f32[16]{0:T(128)S(1)} all-reduce(f32[16]{0:T(128)S(1)} %multiply_reduce_fusion.7), channel_id=1, replica_groups=mesh['patch'=16,'col'=8] {'patch','col'}, use_global_device_ids=true, to_apply=%region_10.0 | all-reduce | flops 16 | bytes 128 | tf_op jit(solution)/shard_map/psum | solution.py:106
  405.3 64.0 %psum.89 = f32[16]{0:T(128)S(1)} all-reduce(f32[16]{0:T(128)S(1)} %multiply_reduce_fusion.6), channel_id=1, replica_groups=mesh['patch'=16,'col'=8] {'patch','col'}, use_global_device_ids=true, to_apply=%region_12.0 | all-reduce | flops 16 | bytes 128 | tf_op jit(solution)/shard_map/psum | solution.py:109
  470.0 3.1 custom-call.12
  473.3 3.0 custom-call.14
  476.7 4.8 collective-permute-start.7
  481.5 14.5 %all_gather.24 = f32[32,16,128]{2,1,0:T(8,128)S(1)} all-gather(f32[4,16,128]{2,1,0:T(8,128)S(1)} %add_add_fusion.1), channel_id=1, replica_groups=mesh['patch'=16,'col'=8] {'col'}, dimensions={0}, use_global_device_ids=true | all-gather | bytes 294912 | tf_op jit(solution)/shard_map/all_gather | solution.py:61
  496.7 7.5 multiply_reduce_fusion.5
  504.2 61.8 %psum.90 = f32[16]{0:T(128)S(1)} all-reduce(f32[16]{0:T(128)S(1)} %get-tuple-element.67), channel_id=1, replica_groups=mesh['patch'=16,'col'=8] {'patch','col'}, use_global_device_ids=true, to_apply=%region_16.0 | all-reduce | flops 16 | bytes 128 | tf_op jit(solution)/shard_map/psum | solution.py:91
  566.6 1.2 collective-permute-start.8
  567.7 3.7 collective-permute-start.9
  571.4 13.9 %all_gather.25 = f32[32,16,128]{2,1,0:T(8,128)S(1)} all-gather(f32[4,16,128]{2,1,0:T(8,128)S(1)} %fusion.45), channel_id=1, replica_groups=mesh['patch'=16,'col'=8] {'col'}, dimensions={0}, use_global_device_ids=true | all-gather | bytes 294912 | tf_op jit(solution)/shard_map/all_gather | solution.py:61
  585.3 0.7 gather_fusion.4
  586.0 7.5 multiply_reduce_fusion.4
  593.5 63.5 %psum.91 = f32[16]{0:T(128)S(1)} all-reduce(f32[16]{0:T(128)S(1)} %get-tuple-element.69), channel_id=1, replica_groups=mesh['patch'=16,'col'=8] {'patch','col'}, use_global_device_ids=true, to_apply=%region_18.0 | all-reduce | flops 16 | bytes 128 | tf_op jit(solution)/shard_map/psum | solution.py:106
  657.1 62.6 %psum.92 = f32[16]{0:T(128)S(1)} all-reduce(f32[16]{0:T(128)S(1)} %multiply_reduce_fusion.3), channel_id=1, replica_groups=mesh['patch'=16,'col'=8] {'patch','col'}, use_global_device_ids=true, to_apply=%region_20.0 | all-reduce | flops 16 | bytes 128 | tf_op jit(solution)/shard_map/psum | solution.py:109
  720.2 0.8 collective-permute-start.10
  721.1 4.0 collective-permute-start.11
  725.0 14.0 %all_gather.26 = f32[32,16,128]{2,1,0:T(8,128)S(1)} all-gather(f32[4,16,128]{2,1,0:T(8,128)S(1)} %fusion.46), channel_id=1, replica_groups=mesh['patch'=16,'col'=8] {'col'}, dimensions={0}, use_global_device_ids=true | all-gather | bytes 294912 | tf_op jit(solution)/shard_map/all_gather | solution.py:61
  739.1 0.7 gather_fusion.5
  739.8 7.5 multiply_reduce_fusion.2
  747.2 64.4 %psum.93 = f32[16]{0:T(128)S(1)} all-reduce(f32[16]{0:T(128)S(1)} %get-tuple-element.71), channel_id=1, replica_groups=mesh['patch'=16,'col'=8] {'patch','col'}, use_global_device_ids=true, to_apply=%region_22.0 | all-reduce | flops 16 | bytes 128 | tf_op jit(solution)/shard_map/psum | solution.py:106
  811.8 62.5 %psum.94 = f32[16]{0:T(128)S(1)} all-reduce(f32[16]{0:T(128)S(1)} %multiply_reduce_fusion.1), channel_id=1, replica_groups=mesh['patch'=16,'col'=8] {'patch','col'}, use_global_device_ids=true, to_apply=%region_24.0 | all-reduce | flops 16 | bytes 128 | tf_op jit(solution)/shard_map/psum | solution.py:106
  874.5 64.0 %psum.95 = f32[16]{0:T(128)S(1)} all-reduce(f32[16]{0:T(128)S(1)} %multiply_reduce_fusion), channel_id=1, replica_groups=mesh['patch'=16,'col'=8] {'patch','col'}, use_global_device_ids=true, to_apply=%region_26.0 | all-reduce | flops 16 | bytes 128 | tf_op jit(solution)/shard_map/psum | solution.py:109
  939.2 3.1 custom-call.15
  942.6 3.0 custom-call.17
  946.0 4.8 collective-permute-start.13
  950.8 14.3 %all_gather.27 = f32[32,16,128]{2,1,0:T(8,128)S(1)} all-gather(f32[4,16,128]{2,1,0:T(8,128)S(1)} %add_add_fusion), channel_id=1, replica_groups=mesh['patch'=16,'col'=8] {'col'}, dimensions={0}, use_global_device_ids=true | all-gather | bytes 294912 | tf_op jit(solution)/shard_map/all_gather | solution.py:61
  965.8 8.0 fusion.3
  (99 shorter events, 8.5 us)
Async XLA Ops:
  0.6 95.9 %copy-start = (f32[4,128,128]{2,1,0:T(8,128)S(1)}, f32[4,128,128]{2,1,0:T(8,128)}, u32[]{:S(2)}) copy-start(f32[4,128,128]{2,1,0:T(8,128)} %param.28) | copy-start | bytes 786436
  0.6 115.9 %copy-start.1 = (f32[4,16,128]{2,1,0:T(8,128)S(1)}, f32[4,16,128]{2,1,0:T(8,128)}, u32[]{:S(2)}) copy-start(f32[4,16,128]{2,1,0:T(8,128)} %param.24) | copy-start | bytes 98308
  0.7 115.9 %copy-start.6 = (f32[4,128]{1,0:T(4,128)S(1)}, f32[4,128]{1,0:T(4,128)}, u32[]{:S(2)}) copy-start(f32[4,128]{1,0:T(4,128)} %param.26) | copy-start | bytes 6148
  0.7 115.9 %copy-start.5 = (f32[4,128]{1,0:T(4,128)S(1)}, f32[4,128]{1,0:T(4,128)}, u32[]{:S(2)}) copy-start(f32[4,128]{1,0:T(4,128)} %param.29) | copy-start | bytes 6148
  0.7 115.9 %copy-start.4 = (f32[4,128]{1,0:T(4,128)S(1)}, f32[4,128]{1,0:T(4,128)}, u32[]{:S(2)}) copy-start(f32[4,128]{1,0:T(4,128)} %param.30) | copy-start | bytes 6148
  0.7 23.3 %collective-permute-start = (f32[4,16,128]{2,1,0:T(8,128)}, f32[4,16,128]{2,1,0:T(8,128)S(1)}, u32[]{:S(2)}, u32[]{:S(2)}) collective-permute-start(f32[4,16,128]{2,1,0:T(8,128)} %param.24), channel_id=1, source_target_pairs={{0,8},{8,16},{16,24},{24,32},{32,40},{40,48},{48,56},{56,64},{64,7... | collective-permute-start | bytes 98312 | tf_op jit(solution)/shard_map/ppermute | solution.py:15
  2.8 21.2 %collective-permute-start.1 = (f32[4,16,128]{2,1,0:T(8,128)}, f32[4,16,128]{2,1,0:T(8,128)S(1)}, u32[]{:S(2)}, u32[]{:S(2)}) collective-permute-start(f32[4,16,128]{2,1,0:T(8,128)} %param.24), channel_id=1, source_target_pairs={{0,120},{8,0},{16,8},{24,16},{32,24},{40,32},{48,40},{56,48},{64,5... | collective-permute-start | bytes 98312 | tf_op jit(solution)/shard_map/ppermute | solution.py:15
  97.1 18.7 %collective-permute-start.2 = (f32[4,16,128]{2,1,0:T(8,128)S(1)}, f32[4,16,128]{2,1,0:T(8,128)S(1)}, u32[]{:S(2)}, u32[]{:S(2)}) collective-permute-start(f32[4,16,128]{2,1,0:T(8,128)S(1)} %fusion.43), channel_id=1, source_target_pairs={{0,8},{8,16},{16,24},{24,32},{32,40},{40,48},{48,56},{56,64},{64,7... | collective-permute-start | bytes 98312 | tf_op jit(solution)/shard_map/ppermute | solution.py:15
  97.3 18.4 %collective-permute-start.3 = (f32[4,16,128]{2,1,0:T(8,128)S(1)}, f32[4,16,128]{2,1,0:T(8,128)S(1)}, u32[]{:S(2)}, u32[]{:S(2)}) collective-permute-start(f32[4,16,128]{2,1,0:T(8,128)S(1)} %fusion.43), channel_id=1, source_target_pairs={{0,120},{8,0},{16,8},{24,16},{32,24},{40,32},{48,40},{56,48},{64,5... | collective-permute-start | bytes 98312 | tf_op jit(solution)/shard_map/ppermute | solution.py:15
  251.2 18.6 %collective-permute-start.4 = (f32[4,16,128]{2,1,0:T(8,128)S(1)}, f32[4,16,128]{2,1,0:T(8,128)S(1)}, u32[]{:S(2)}, u32[]{:S(2)}) collective-permute-start(f32[4,16,128]{2,1,0:T(8,128)S(1)} %fusion.44), channel_id=1, source_target_pairs={{0,8},{8,16},{16,24},{24,32},{32,40},{40,48},{48,56},{56,64},{64,7... | collective-permute-start | bytes 98312 | tf_op jit(solution)/shard_map/ppermute | solution.py:15
  252.1 17.7 %collective-permute-start.5 = (f32[4,16,128]{2,1,0:T(8,128)S(1)}, f32[4,16,128]{2,1,0:T(8,128)S(1)}, u32[]{:S(2)}, u32[]{:S(2)}) collective-permute-start(f32[4,16,128]{2,1,0:T(8,128)S(1)} %fusion.44), channel_id=1, source_target_pairs={{0,120},{8,0},{16,8},{24,16},{32,24},{40,32},{48,40},{56,48},{64,5... | collective-permute-start | bytes 98312 | tf_op jit(solution)/shard_map/ppermute | solution.py:15
  269.8 226.9 %copy-start.2 = (f32[4,16,128]{2,1,0:T(8,128)S(1)}, f32[4,16,128]{2,1,0:T(8,128)}, u32[]{:S(2)}) copy-start(f32[4,16,128]{2,1,0:T(8,128)} %param.25) | copy-start | bytes 98308
  476.7 19.3 %collective-permute-start.6 = (f32[4,16,128]{2,1,0:T(8,128)S(1)}, f32[4,16,128]{2,1,0:T(8,128)S(1)}, u32[]{:S(2)}, u32[]{:S(2)}) collective-permute-start(f32[4,16,128]{2,1,0:T(8,128)S(1)} %add_add_fusion.1), channel_id=1, source_target_pairs={{0,8},{8,16},{16,24},{24,32},{32,40},{40,48},{48,56},{56,64},{64,7... | collective-permute-start | bytes 98312 | tf_op jit(solution)/shard_map/ppermute | solution.py:15
  476.7 19.3 %collective-permute-start.7 = (f32[4,16,128]{2,1,0:T(8,128)S(1)}, f32[4,16,128]{2,1,0:T(8,128)S(1)}, u32[]{:S(2)}, u32[]{:S(2)}) collective-permute-start(f32[4,16,128]{2,1,0:T(8,128)S(1)} %add_add_fusion.1), channel_id=1, source_target_pairs={{0,120},{8,0},{16,8},{24,16},{32,24},{40,32},{48,40},{56,48},{64,5... | collective-permute-start | bytes 98312 | tf_op jit(solution)/shard_map/ppermute | solution.py:15
  566.6 18.7 %collective-permute-start.8 = (f32[4,16,128]{2,1,0:T(8,128)S(1)}, f32[4,16,128]{2,1,0:T(8,128)S(1)}, u32[]{:S(2)}, u32[]{:S(2)}) collective-permute-start(f32[4,16,128]{2,1,0:T(8,128)S(1)} %fusion.45), channel_id=1, source_target_pairs={{0,8},{8,16},{16,24},{24,32},{32,40},{40,48},{48,56},{56,64},{64,7... | collective-permute-start | bytes 98312 | tf_op jit(solution)/shard_map/ppermute | solution.py:15
  567.7 17.5 %collective-permute-start.9 = (f32[4,16,128]{2,1,0:T(8,128)S(1)}, f32[4,16,128]{2,1,0:T(8,128)S(1)}, u32[]{:S(2)}, u32[]{:S(2)}) collective-permute-start(f32[4,16,128]{2,1,0:T(8,128)S(1)} %fusion.45), channel_id=1, source_target_pairs={{0,120},{8,0},{16,8},{24,16},{32,24},{40,32},{48,40},{56,48},{64,5... | collective-permute-start | bytes 98312 | tf_op jit(solution)/shard_map/ppermute | solution.py:15
  720.2 18.8 %collective-permute-start.10 = (f32[4,16,128]{2,1,0:T(8,128)S(1)}, f32[4,16,128]{2,1,0:T(8,128)S(1)}, u32[]{:S(2)}, u32[]{:S(2)}) collective-permute-start(f32[4,16,128]{2,1,0:T(8,128)S(1)} %fusion.46), channel_id=1, source_target_pairs={{0,8},{8,16},{16,24},{24,32},{32,40},{40,48},{48,56},{56,64},{64,7... | collective-permute-start | bytes 98312 | tf_op jit(solution)/shard_map/ppermute | solution.py:15
  721.1 17.9 %collective-permute-start.11 = (f32[4,16,128]{2,1,0:T(8,128)S(1)}, f32[4,16,128]{2,1,0:T(8,128)S(1)}, u32[]{:S(2)}, u32[]{:S(2)}) collective-permute-start(f32[4,16,128]{2,1,0:T(8,128)S(1)} %fusion.46), channel_id=1, source_target_pairs={{0,120},{8,0},{16,8},{24,16},{32,24},{40,32},{48,40},{56,48},{64,5... | collective-permute-start | bytes 98312 | tf_op jit(solution)/shard_map/ppermute | solution.py:15
  945.9 27.9 %copy-start.3 = (f32[4,16,128]{2,1,0:T(8,128)}, f32[4,16,128]{2,1,0:T(8,128)S(1)}, u32[]{:S(2)}) copy-start(f32[4,16,128]{2,1,0:T(8,128)S(1)} %add_add_fusion) | copy-start | bytes 98308
  945.9 19.2 %collective-permute-start.12 = (f32[4,16,128]{2,1,0:T(8,128)S(1)}, f32[4,16,128]{2,1,0:T(8,128)S(1)}, u32[]{:S(2)}, u32[]{:S(2)}) collective-permute-start(f32[4,16,128]{2,1,0:T(8,128)S(1)} %add_add_fusion), channel_id=1, source_target_pairs={{0,8},{8,16},{16,24},{24,32},{32,40},{40,48},{48,56},{56,64},{64,7... | collective-permute-start | bytes 98312 | tf_op jit(solution)/shard_map/ppermute | solution.py:15
  946.0 19.1 %collective-permute-start.13 = (f32[4,16,128]{2,1,0:T(8,128)S(1)}, f32[4,16,128]{2,1,0:T(8,128)S(1)}, u32[]{:S(2)}, u32[]{:S(2)}) collective-permute-start(f32[4,16,128]{2,1,0:T(8,128)S(1)} %add_add_fusion), channel_id=1, source_target_pairs={{0,120},{8,0},{16,8},{24,16},{32,24},{40,32},{48,40},{56,48},{64,5... | collective-permute-start | bytes 98312 | tf_op jit(solution)/shard_map/ppermute | solution.py:15
where the time goes:
time: 984 us; the launch traced here: 974 us
  blocking collectives  860 us (87%)
  matrix products  55.7 us (6%)
  starting transfers between devices  34.8 us (4%)
  other arithmetic  16.5 us (2%)
    psum x6, blocking collectives, body(): coeff = lax.psum(column_sum(basis[place], image), ('patch', 'col'))  381 us
    psum x4, blocking collectives, body(): norm = jnp.sqrt(lax.psum(column_sum(image, image), ('patch', 'col')) + EPS)  254 us
    psum x2, blocking collectives, body(): beta = jnp.sqrt(lax.psum(column_sum(start, start), ('patch', 'col')) + EPS)  126 us
    all_gather x7, blocking collectives, near_field(): own_patch = lax.all_gather(field, 'col', axis=0, tiled=True)  99.4 us
    dot_general x7, matrix products, near_field(): jnp.einsum('bkij,bkcj->bci', nearfield, sources * live_mask[:, :, None, N...  52.9 us
    ppermute x14, starting transfers between devices, from_behind(): lax.ppermute(array, axis, [(i, (i + by) % size) for i in range(size)])  34.8 us
  transfers between devices with their start and end apart: 14, of which 0 were waited for; matrix products, arithmetic and copies ran while one was open for 0% of the time, Pallas kernels for 0%

commit v1 on v0

--- a/solution.py
+++ b/solution.py
@@ -2,6 +2,7 @@
 import jax.numpy as jnp
 from jax import lax
 from jax.sharding import PartitionSpec as P
+from jax.lax import psum
 
 NEWTON = 2
 GMRES = 2
@@ -88,7 +89,7 @@
     for newton in range(NEWTON):
         value, slope = mismatch(field, near_now)
         start = -value
-        beta = jnp.sqrt(lax.psum(column_sum(start, start), ("patch", "col")) + EPS)
+        beta = jnp.sqrt(psum(psum(column_sum(start, start), "col"), "patch") + EPS)
         basis = [start / beta[None, :, None]]
         directions = []
         near_images = []

time: 984 us -> 953 us (0.968)
  blocking collectives: 860 us -> 829 us
    psum x2 -> x4, blocking collectives: 126 us -> 82.5 us  [body(): beta = jnp.sqrt(psum(psum(column_sum(start, start), 'col'), 'patch') + EPS)]
    all_gather x7, blocking collectives: 99.4 us -> 117 us  [near_field(): own_patch = lax.all_gather(field, 'col', axis=0, tiled=True)]
where the time goes in v1:
time: 953 us; the launch traced here: 943 us
  blocking collectives  829 us (87%)
  matrix products  55.7 us (6%)
  starting transfers between devices  34.9 us (4%)
  other arithmetic  16.5 us (2%)
    psum x6, blocking collectives, body(): coeff = lax.psum(column_sum(basis[place], image), ('patch', 'col'))  374 us
    psum x4, blocking collectives, body(): norm = jnp.sqrt(lax.psum(column_sum(image, image), ('patch', 'col')) + EPS)  255 us
    all_gather x7, blocking collectives, near_field(): own_patch = lax.all_gather(field, 'col', axis=0, tiled=True)  117 us
    psum x4, blocking collectives, body(): beta = jnp.sqrt(psum(psum(column_sum(start, start), 'col'), 'patch') + EPS)  82.5 us
    dot_general x7, matrix products, near_field(): jnp.einsum('bkij,bkcj->bci', nearfield, sources * live_mask[:, :, None, N...  52.9 us
    ppermute x14, starting transfers between devices, from_behind(): lax.ppermute(array, axis, [(i, (i + by) % size) for i in range(size)])  34.9 us
  transfers between devices with their start and end apart: 14, of which 0 were waited for; matrix products, arithmetic and copies ran while one was open for 0% of the time, Pallas kernels for 0%

profile of v1, /device:TPU:1, one launch (start us, length us, event | category | flops | bytes accessed | tf_op | source)
XLA Modules:
  0.0 943.2 jit_solution(5481530788613409336)
XLA Ops:
  0.7 2.1 collective-permute-start
  2.8 3.8 collective-permute-start.1
  6.6 15.1 %all_gather.21 = f32[32,16,128]{2,1,0:T(8,128)S(1)} all-gather(f32[4,16,128]{2,1,0:T(8,128)} %param.24), channel_id=1, replica_groups=mesh['patch'=16,'col'=8] {'col'}, dimensions={0}, use_global_device_ids=true | all-gather | bytes 294912 | tf_op jit(solution)/shard_map/all_gather | solution.py:62
  22.5 0.7 fusion.40
  23.2 0.8 select_reduce_fusion
  24.0 0.7 gather_fusion
  24.7 7.6 multiply_reduce_fusion.11
  32.3 11.9 %psum.98 = f32[16]{0:T(128)S(1)} all-reduce(f32[16]{0:T(128)S(1)} %get-tuple-element.61), channel_id=1, replica_groups=mesh['patch'=16,'col'=8] {'col'}, use_global_device_ids=true, to_apply=%region_2.0 | all-reduce | flops 16 | bytes 128 | tf_op jit(solution)/shard_map/psum | solution.py:92
  44.2 30.1 %psum.99 = f32[16]{0:T(128)S(1)} all-reduce(f32[16]{0:T(128)S(1)} %psum.98), channel_id=1, replica_groups=mesh['patch'=16,'col'=8] {'patch'}, use_global_device_ids=true, to_apply=%region_3.0 | all-reduce | flops 16 | bytes 128 | tf_op jit(solution)/shard_map/psum | solution.py:92
  74.9 4.8 collective-permute-start.3
  79.7 23.9 %all_gather.22 = f32[32,16,128]{2,1,0:T(8,128)S(1)} all-gather(f32[4,16,128]{2,1,0:T(8,128)S(1)} %fusion.43), channel_id=1, replica_groups=mesh['patch'=16,'col'=8] {'col'}, dimensions={0}, use_global_device_ids=true | all-gather | bytes 294912 | tf_op jit(solution)/shard_map/all_gather | solution.py:62
  103.6 0.7 gather_fusion.1
  104.3 7.5 multiply_reduce_fusion.10
  111.8 61.8 %psum.100 = f32[16]{0:T(128)S(1)} all-reduce(f32[16]{0:T(128)S(1)} %get-tuple-element.63), channel_id=1, replica_groups=mesh['patch'=16,'col'=8] {'patch','col'}, use_global_device_ids=true, to_apply=%region_5.0 | all-reduce | flops 16 | bytes 128 | tf_op jit(solution)/shard_map/psum | solution.py:107
  173.8 63.5 %psum.101 = f32[16]{0:T(128)S(1)} all-reduce(f32[16]{0:T(128)S(1)} %multiply_reduce_fusion.9), channel_id=1, replica_groups=mesh['patch'=16,'col'=8] {'patch','col'}, use_global_device_ids=true, to_apply=%region_7.0 | all-reduce | flops 16 | bytes 128 | tf_op jit(solution)/shard_map/psum | solution.py:110
  238.0 4.7 collective-permute-start.5
  242.7 14.6 %all_gather.23 = f32[32,16,128]{2,1,0:T(8,128)S(1)} all-gather(f32[4,16,128]{2,1,0:T(8,128)S(1)} %fusion.44), channel_id=1, replica_groups=mesh['patch'=16,'col'=8] {'col'}, dimensions={0}, use_global_device_ids=true | all-gather | bytes 294912 | tf_op jit(solution)/shard_map/all_gather | solution.py:62
  258.0 7.5 multiply_reduce_fusion.8
  265.5 62.4 %psum.102 = f32[16]{0:T(128)S(1)} all-reduce(f32[16]{0:T(128)S(1)} %get-tuple-element.65), channel_id=1, replica_groups=mesh['patch'=16,'col'=8] {'patch','col'}, use_global_device_ids=true, to_apply=%region_9.0 | all-reduce | flops 16 | bytes 128 | tf_op jit(solution)/shard_map/psum | solution.py:107
  328.1 62.9 %psum.103 = f32[16]{0:T(128)S(1)} all-reduce(f32[16]{0:T(128)S(1)} %multiply_reduce_fusion.7), channel_id=1, replica_groups=mesh['patch'=16,'col'=8] {'patch','col'}, use_global_device_ids=true, to_apply=%region_11.0 | all-reduce | flops 16 | bytes 128 | tf_op jit(solution)/shard_map/psum | solution.py:107
  391.2 63.8 %psum.104 = f32[16]{0:T(128)S(1)} all-reduce(f32[16]{0:T(128)S(1)} %multiply_reduce_fusion.6), channel_id=1, replica_groups=mesh['patch'=16,'col'=8] {'patch','col'}, use_global_device_ids=true, to_apply=%region_13.0 | all-reduce | flops 16 | bytes 128 | tf_op jit(solution)/shard_map/psum | solution.py:110
  455.6 3.1 custom-call.12
  459.0 3.0 custom-call.14
  462.3 4.8 collective-permute-start.7
  467.1 14.1 %all_gather.24 = f32[32,16,128]{2,1,0:T(8,128)S(1)} all-gather(f32[4,16,128]{2,1,0:T(8,128)S(1)} %add_add_fusion.1), channel_id=1, replica_groups=mesh['patch'=16,'col'=8] {'col'}, dimensions={0}, use_global_device_ids=true | all-gather | bytes 294912 | tf_op jit(solution)/shard_map/all_gather | solution.py:62
  482.0 7.5 multiply_reduce_fusion.5
  489.5 11.9 %psum.105 = f32[16]{0:T(128)S(1)} all-reduce(f32[16]{0:T(128)S(1)} %get-tuple-element.67), channel_id=1, replica_groups=mesh['patch'=16,'col'=8] {'col'}, use_global_device_ids=true, to_apply=%region_17.0 | all-reduce | flops 16 | bytes 128 | tf_op jit(solution)/shard_map/psum | solution.py:92
  501.4 28.5 %psum.106 = f32[16]{0:T(128)S(1)} all-reduce(f32[16]{0:T(128)S(1)} %psum.105), channel_id=1, replica_groups=mesh['patch'=16,'col'=8] {'patch'}, use_global_device_ids=true, to_apply=%region_18.0 | all-reduce | flops 16 | bytes 128 | tf_op jit(solution)/shard_map/psum | solution.py:92
  530.5 1.7 collective-permute-start.8
  532.2 3.2 collective-permute-start.9
  535.4 21.4 %all_gather.25 = f32[32,16,128]{2,1,0:T(8,128)S(1)} all-gather(f32[4,16,128]{2,1,0:T(8,128)S(1)} %fusion.45), channel_id=1, replica_groups=mesh['patch'=16,'col'=8] {'col'}, dimensions={0}, use_global_device_ids=true | all-gather | bytes 294912 | tf_op jit(solution)/shard_map/all_gather | solution.py:62
  556.8 0.7 gather_fusion.4
  557.5 7.5 multiply_reduce_fusion.4
  565.0 61.8 %psum.107 = f32[16]{0:T(128)S(1)} all-reduce(f32[16]{0:T(128)S(1)} %get-tuple-element.69), channel_id=1, replica_groups=mesh['patch'=16,'col'=8] {'patch','col'}, use_global_device_ids=true, to_apply=%region_20.0 | all-reduce | flops 16 | bytes 128 | tf_op jit(solution)/shard_map/psum | solution.py:107
  627.0 63.5 %psum.108 = f32[16]{0:T(128)S(1)} all-reduce(f32[16]{0:T(128)S(1)} %multiply_reduce_fusion.3), channel_id=1, replica_groups=mesh['patch'=16,'col'=8] {'patch','col'}, use_global_device_ids=true, to_apply=%region_22.0 | all-reduce | flops 16 | bytes 128 | tf_op jit(solution)/shard_map/psum | solution.py:110
  691.2 4.7 collective-permute-start.11
  695.8 14.1 %all_gather.26 = f32[32,16,128]{2,1,0:T(8,128)S(1)} all-gather(f32[4,16,128]{2,1,0:T(8,128)S(1)} %fusion.46), channel_id=1, replica_groups=mesh['patch'=16,'col'=8] {'col'}, dimensions={0}, use_global_device_ids=true | all-gather | bytes 294912 | tf_op jit(solution)/shard_map/all_gather | solution.py:62
  710.0 0.7 gather_fusion.5
  710.7 7.5 multiply_reduce_fusion.2
  718.2 62.4 %psum.109 = f32[16]{0:T(128)S(1)} all-reduce(f32[16]{0:T(128)S(1)} %get-tuple-element.71), channel_id=1, replica_groups=mesh['patch'=16,'col'=8] {'patch','col'}, use_global_device_ids=true, to_apply=%region_24.0 | all-reduce | flops 16 | bytes 128 | tf_op jit(solution)/shard_map/psum | solution.py:107
  780.8 63.1 %psum.110 = f32[16]{0:T(128)S(1)} all-reduce(f32[16]{0:T(128)S(1)} %multiply_reduce_fusion.1), channel_id=1, replica_groups=mesh['patch'=16,'col'=8] {'patch','col'}, use_global_device_ids=true, to_apply=%region_26.0 | all-reduce | flops 16 | bytes 128 | tf_op jit(solution)/shard_map/psum | solution.py:107
  844.1 63.8 %psum.111 = f32[16]{0:T(128)S(1)} all-reduce(f32[16]{0:T(128)S(1)} %multiply_reduce_fusion), channel_id=1, replica_groups=mesh['patch'=16,'col'=8] {'patch','col'}, use_global_device_ids=true, to_apply=%region_28.0 | all-reduce | flops 16 | bytes 128 | tf_op jit(solution)/shard_map/psum | solution.py:110
  908.5 3.1 custom-call.15
  911.9 3.0 custom-call.17
  915.3 4.8 collective-permute-start.13
  920.1 14.1 %all_gather.27 = f32[32,16,128]{2,1,0:T(8,128)S(1)} all-gather(f32[4,16,128]{2,1,0:T(8,128)S(1)} %add_add_fusion), channel_id=1, replica_groups=mesh['patch'=16,'col'=8] {'col'}, dimensions={0}, use_global_device_ids=true | all-gather | bytes 294912 | tf_op jit(solution)/shard_map/all_gather | solution.py:62
  934.2 0.7 gather_fusion.6
  934.9 8.0 fusion.3
  (101 shorter events, 8.5 us)
Async XLA Ops:
  0.6 73.7 %copy-start = (f32[4,128,128]{2,1,0:T(8,128)S(1)}, f32[4,128,128]{2,1,0:T(8,128)}, u32[]{:S(2)}) copy-start(f32[4,128,128]{2,1,0:T(8,128)} %param.28) | copy-start | bytes 786436
  0.6 103.7 %copy-start.1 = (f32[4,16,128]{2,1,0:T(8,128)S(1)}, f32[4,16,128]{2,1,0:T(8,128)}, u32[]{:S(2)}) copy-start(f32[4,16,128]{2,1,0:T(8,128)} %param.24) | copy-start | bytes 98308
  0.7 103.7 %copy-start.6 = (f32[4,128]{1,0:T(4,128)S(1)}, f32[4,128]{1,0:T(4,128)}, u32[]{:S(2)}) copy-start(f32[4,128]{1,0:T(4,128)} %param.26) | copy-start | bytes 6148
  0.7 103.7 %copy-start.5 = (f32[4,128]{1,0:T(4,128)S(1)}, f32[4,128]{1,0:T(4,128)}, u32[]{:S(2)}) copy-start(f32[4,128]{1,0:T(4,128)} %param.29) | copy-start | bytes 6148
  0.7 103.7 %copy-start.4 = (f32[4,128]{1,0:T(4,128)S(1)}, f32[4,128]{1,0:T(4,128)}, u32[]{:S(2)}) copy-start(f32[4,128]{1,0:T(4,128)} %param.30) | copy-start | bytes 6148
  0.7 23.3 %collective-permute-start = (f32[4,16,128]{2,1,0:T(8,128)}, f32[4,16,128]{2,1,0:T(8,128)S(1)}, u32[]{:S(2)}, u32[]{:S(2)}) collective-permute-start(f32[4,16,128]{2,1,0:T(8,128)} %param.24), channel_id=1, source_target_pairs={{0,8},{8,16},{16,24},{24,32},{32,40},{40,48},{48,56},{56,64},{64,7... | collective-permute-start | bytes 98312 | tf_op jit(solution)/shard_map/ppermute | solution.py:16
  2.8 21.2 %collective-permute-start.1 = (f32[4,16,128]{2,1,0:T(8,128)}, f32[4,16,128]{2,1,0:T(8,128)S(1)}, u32[]{:S(2)}, u32[]{:S(2)}) collective-permute-start(f32[4,16,128]{2,1,0:T(8,128)} %param.24), channel_id=1, source_target_pairs={{0,120},{8,0},{16,8},{24,16},{32,24},{40,32},{48,40},{56,48},{64,5... | collective-permute-start | bytes 98312 | tf_op jit(solution)/shard_map/ppermute | solution.py:16
  74.9 28.7 %collective-permute-start.2 = (f32[4,16,128]{2,1,0:T(8,128)S(1)}, f32[4,16,128]{2,1,0:T(8,128)S(1)}, u32[]{:S(2)}, u32[]{:S(2)}) collective-permute-start(f32[4,16,128]{2,1,0:T(8,128)S(1)} %fusion.43), channel_id=1, source_target_pairs={{0,8},{8,16},{16,24},{24,32},{32,40},{40,48},{48,56},{56,64},{64,7... | collective-permute-start | bytes 98312 | tf_op jit(solution)/shard_map/ppermute | solution.py:16
  74.9 28.6 %collective-permute-start.3 = (f32[4,16,128]{2,1,0:T(8,128)S(1)}, f32[4,16,128]{2,1,0:T(8,128)S(1)}, u32[]{:S(2)}, u32[]{:S(2)}) collective-permute-start(f32[4,16,128]{2,1,0:T(8,128)S(1)} %fusion.43), channel_id=1, source_target_pairs={{0,120},{8,0},{16,8},{24,16},{32,24},{40,32},{48,40},{56,48},{64,5... | collective-permute-start | bytes 98312 | tf_op jit(solution)/shard_map/ppermute | solution.py:16
  237.9 19.4 %collective-permute-start.4 = (f32[4,16,128]{2,1,0:T(8,128)S(1)}, f32[4,16,128]{2,1,0:T(8,128)S(1)}, u32[]{:S(2)}, u32[]{:S(2)}) collective-permute-start(f32[4,16,128]{2,1,0:T(8,128)S(1)} %fusion.44), channel_id=1, source_target_pairs={{0,8},{8,16},{16,24},{24,32},{32,40},{40,48},{48,56},{56,64},{64,7... | collective-permute-start | bytes 98312 | tf_op jit(solution)/shard_map/ppermute | solution.py:16
  238.0 19.3 %collective-permute-start.5 = (f32[4,16,128]{2,1,0:T(8,128)S(1)}, f32[4,16,128]{2,1,0:T(8,128)S(1)}, u32[]{:S(2)}, u32[]{:S(2)}) collective-permute-start(f32[4,16,128]{2,1,0:T(8,128)S(1)} %fusion.44), channel_id=1, source_target_pairs={{0,120},{8,0},{16,8},{24,16},{32,24},{40,32},{48,40},{56,48},{64,5... | collective-permute-start | bytes 98312 | tf_op jit(solution)/shard_map/ppermute | solution.py:16
  257.3 224.7 %copy-start.2 = (f32[4,16,128]{2,1,0:T(8,128)S(1)}, f32[4,16,128]{2,1,0:T(8,128)}, u32[]{:S(2)}) copy-start(f32[4,16,128]{2,1,0:T(8,128)} %param.25) | copy-start | bytes 98308
  462.3 18.9 %collective-permute-start.6 = (f32[4,16,128]{2,1,0:T(8,128)S(1)}, f32[4,16,128]{2,1,0:T(8,128)S(1)}, u32[]{:S(2)}, u32[]{:S(2)}) collective-permute-start(f32[4,16,128]{2,1,0:T(8,128)S(1)} %add_add_fusion.1), channel_id=1, source_target_pairs={{0,8},{8,16},{16,24},{24,32},{32,40},{40,48},{48,56},{56,64},{64,7... | collective-permute-start | bytes 98312 | tf_op jit(solution)/shard_map/ppermute | solution.py:16
  462.3 18.9 %collective-permute-start.7 = (f32[4,16,128]{2,1,0:T(8,128)S(1)}, f32[4,16,128]{2,1,0:T(8,128)S(1)}, u32[]{:S(2)}, u32[]{:S(2)}) collective-permute-start(f32[4,16,128]{2,1,0:T(8,128)S(1)} %add_add_fusion.1), channel_id=1, source_target_pairs={{0,120},{8,0},{16,8},{24,16},{32,24},{40,32},{48,40},{56,48},{64,5... | collective-permute-start | bytes 98312 | tf_op jit(solution)/shard_map/ppermute | solution.py:16
  530.5 26.3 %collective-permute-start.8 = (f32[4,16,128]{2,1,0:T(8,128)S(1)}, f32[4,16,128]{2,1,0:T(8,128)S(1)}, u32[]{:S(2)}, u32[]{:S(2)}) collective-permute-start(f32[4,16,128]{2,1,0:T(8,128)S(1)} %fusion.45), channel_id=1, source_target_pairs={{0,8},{8,16},{16,24},{24,32},{32,40},{40,48},{48,56},{56,64},{64,7... | collective-permute-start | bytes 98312 | tf_op jit(solution)/shard_map/ppermute | solution.py:16
  532.2 24.6 %collective-permute-start.9 = (f32[4,16,128]{2,1,0:T(8,128)S(1)}, f32[4,16,128]{2,1,0:T(8,128)S(1)}, u32[]{:S(2)}, u32[]{:S(2)}) collective-permute-start(f32[4,16,128]{2,1,0:T(8,128)S(1)} %fusion.45), channel_id=1, source_target_pairs={{0,120},{8,0},{16,8},{24,16},{32,24},{40,32},{48,40},{56,48},{64,5... | collective-permute-start | bytes 98312 | tf_op jit(solution)/shard_map/ppermute | solution.py:16
  691.0 19.0 %collective-permute-start.10 = (f32[4,16,128]{2,1,0:T(8,128)S(1)}, f32[4,16,128]{2,1,0:T(8,128)S(1)}, u32[]{:S(2)}, u32[]{:S(2)}) collective-permute-start(f32[4,16,128]{2,1,0:T(8,128)S(1)} %fusion.46), channel_id=1, source_target_pairs={{0,8},{8,16},{16,24},{24,32},{32,40},{40,48},{48,56},{56,64},{64,7... | collective-permute-start | bytes 98312 | tf_op jit(solution)/shard_map/ppermute | solution.py:16
  691.2 18.8 %collective-permute-start.11 = (f32[4,16,128]{2,1,0:T(8,128)S(1)}, f32[4,16,128]{2,1,0:T(8,128)S(1)}, u32[]{:S(2)}, u32[]{:S(2)}) collective-permute-start(f32[4,16,128]{2,1,0:T(8,128)S(1)} %fusion.46), channel_id=1, source_target_pairs={{0,120},{8,0},{16,8},{24,16},{32,24},{40,32},{48,40},{56,48},{64,5... | collective-permute-start | bytes 98312 | tf_op jit(solution)/shard_map/ppermute | solution.py:16
  915.2 27.7 %copy-start.3 = (f32[4,16,128]{2,1,0:T(8,128)}, f32[4,16,128]{2,1,0:T(8,128)S(1)}, u32[]{:S(2)}) copy-start(f32[4,16,128]{2,1,0:T(8,128)S(1)} %add_add_fusion) | copy-start | bytes 98308
  915.2 19.0 %collective-permute-start.12 = (f32[4,16,128]{2,1,0:T(8,128)S(1)}, f32[4,16,128]{2,1,0:T(8,128)S(1)}, u32[]{:S(2)}, u32[]{:S(2)}) collective-permute-start(f32[4,16,128]{2,1,0:T(8,128)S(1)} %add_add_fusion), channel_id=1, source_target_pairs={{0,8},{8,16},{16,24},{24,32},{32,40},{40,48},{48,56},{56,64},{64,7... | collective-permute-start | bytes 98312 | tf_op jit(solution)/shard_map/ppermute | solution.py:16
  915.3 18.9 %collective-permute-start.13 = (f32[4,16,128]{2,1,0:T(8,128)S(1)}, f32[4,16,128]{2,1,0:T(8,128)S(1)}, u32[]{:S(2)}, u32[]{:S(2)}) collective-permute-start(f32[4,16,128]{2,1,0:T(8,128)S(1)} %add_add_fusion), channel_id=1, source_target_pairs={{0,120},{8,0},{16,8},{24,16},{32,24},{40,32},{48,40},{56,48},{64,5... | collective-permute-start | bytes 98312 | tf_op jit(solution)/shard_map/ppermute | solution.py:16
